TPU v7x, 32 devices: a whole 2x2x4 slice. The times are simulated.
32 devices in a mesh: groups: 2 (over y), blk: 4 (over z), head: 4 (over x, core).
Axes of the slice: x: 2, y: 2, z: 4, core: 2. Of those that a mesh axis runs over, the one named last changes fastest.
Arguments:
- queries: bfloat16 [4, 4, 8192], P('groups', 'blk', 'head'), parts along dimension 0, may hold values from -4.5 to 4.5
- stored_cache_keys: bfloat16 [4, 2048, 1024], P('groups', 'blk', 'head'), parts along dimension 0, may hold values from -4.5 to 4.5
- stored_cache_values: bfloat16 [4, 2048, 1024], P('groups', 'blk', 'head'), parts along dimension 0, may hold values from -6 to 6
- out_weight: bfloat16 [8192, 8192], P('head', 'blk'), may hold values from -3 to 3
- lengths: int32 [4], P('groups'), parts along dimension 0, may hold values from 1024 to 2048
Outputs:
- projected: bfloat16 [4, 4, 8192], P('groups', 'head', 'blk'), parts along dimension 0
There are 2 independent parts, one for each index of `groups`. A program takes and returns all parts, laid end to end along the dimension named above; an argument that names none is the same for every part. Nothing has to cross between parts.
All inputs are finite; a program needn't handle non-finite values.
Results may differ from a plain program's by a relative error of at most 0.0056.
Values may be sent and summed in bfloat16 or wider, within the bound.
A program may use at most 64 MiB of HBM per device.

v0:
```python
import math

import jax
import jax.numpy as jnp
from jax import lax
from jax.sharding import PartitionSpec as P

REQUEST_COUNT = 2
QUERY_HEAD_COUNT = 64
KEY_VALUE_HEADS = 8
HEAD_DIMENSION = 128


masked_fill_value = -1e30


def body(queries, stored_cache_keys, stored_cache_values, out_weight, lengths):
    group_width = QUERY_HEAD_COUNT // KEY_VALUE_HEADS
    local_heads = stored_cache_keys.shape[2] // HEAD_DIMENSION
    query_heads = local_heads * group_width
    span = stored_cache_keys.shape[1]
    new_count = queries.shape[1] * lax.axis_size("blk")
    key_pos = lax.axis_index("blk") * span + jnp.arange(span, dtype=jnp.int32)
    score_scale = 1.0 / math.sqrt(HEAD_DIMENSION)
    piece = lax.all_gather(queries, "blk", axis=1, tiled=True)
    rows_count = piece.shape[1]
    query_pos = lengths[:, None] - new_count + jnp.arange(rows_count, dtype=jnp.int32)[None, :]
    sums_list = []
    maxima_list = []
    totals_list = []
    for request in range(REQUEST_COUNT):
        visible = (key_pos[None, :] <= query_pos[request][:, None])[:, None, :]
        parts_sum, parts_max, parts_total = ([], [], [])
        for kv_head in range(local_heads):
            block_query = piece[
                request,
                :,
                kv_head
                * group_width
                * HEAD_DIMENSION : (kv_head + 1)
                * group_width
                * HEAD_DIMENSION,
            ].reshape(rows_count, group_width, HEAD_DIMENSION)
            local_keys = stored_cache_keys[
                request, :, kv_head * HEAD_DIMENSION : (kv_head + 1) * HEAD_DIMENSION
            ]
            local_values = stored_cache_values[
                request, :, kv_head * HEAD_DIMENSION : (kv_head + 1) * HEAD_DIMENSION
            ]
            scores = (
                jnp.einsum(
                    "ngd,cd->ngc", block_query, local_keys, preferred_element_type=jnp.float32
                )
                * score_scale
            )
            block_max = jnp.max(jnp.where(visible, scores, masked_fill_value), axis=-1)
            weights = jnp.where(visible, jnp.exp(scores - block_max[..., None]), 0.0)
            parts_total.append(jnp.sum(weights, axis=-1))
            parts_max.append(block_max)
            weighted = jnp.einsum(
                "ngc,cd->ngd",
                weights.astype(jnp.bfloat16),
                local_values,
                preferred_element_type=jnp.float32,
            )
            parts_sum.append(weighted.reshape(rows_count, group_width * HEAD_DIMENSION))
        sums_list.append(jnp.concatenate(parts_sum, axis=1))
        maxima_list.append(jnp.concatenate(parts_max, axis=1))
        totals_list.append(jnp.concatenate(parts_total, axis=1))
    new_sums = jnp.stack(sums_list, axis=0)
    new_maxima = jnp.stack(maxima_list, axis=0)
    new_totals = jnp.stack(totals_list, axis=0)
    received = (
        lax.all_to_all(new_sums[None], "blk", split_axis=2, concat_axis=0, tiled=True),
        lax.all_to_all(new_maxima[None], "blk", split_axis=2, concat_axis=0, tiled=True),
        lax.all_to_all(new_totals[None], "blk", split_axis=2, concat_axis=0, tiled=True),
    )
    part_sums, part_max, part_totals = received
    blocks = part_sums.shape[0]
    own_rows = part_sums.shape[2]
    top = jnp.max(part_max, axis=0)
    factor = jnp.exp(part_max - top[None])
    overall = jnp.sum(factor * part_totals, axis=0)
    shaped = part_sums.reshape(blocks, REQUEST_COUNT, own_rows, query_heads, HEAD_DIMENSION)
    merged = jnp.sum(shaped * factor[..., None], axis=0) / overall[..., None]
    own_attention = merged.astype(jnp.bfloat16).reshape(
        REQUEST_COUNT, own_rows, query_heads * HEAD_DIMENSION
    )
    terms = jnp.einsum(
        "rnc,cd->rnd",
        lax.all_gather(own_attention, "blk", axis=1, tiled=True),
        out_weight,
        preferred_element_type=jnp.float32,
    )
    return lax.psum_scatter(terms, "head", scatter_dimension=1, tiled=True).astype(jnp.bfloat16)


def solution(mesh):
    placed = (
        P("groups", "blk", "head"),
        P("groups", "blk", "head"),
        P("groups", "blk", "head"),
        P("head", "blk"),
        P("groups"),
    )
    return jax.shard_map(
        body, mesh=mesh, in_specs=placed, out_specs=P("groups", "head", "blk"), check_vma=False
    )
```

profile of v0, /device:TPU:0, one launch (start us, length us, event | category | flops | bytes accessed | tf_op | source)
XLA Modules:
  0.0 82.9 jit_solution(6853491526789684254)
XLA Ops:
  0.0 0.7 broadcast_add_fusion
  0.7 0.1 iota_add_fusion.1
  0.7 15.0 %all_gather.6 = bf16[2,4,2048]{2,0,1:T(2,128)(2,1)S(1)} all-gather(bf16[2,1,2048]{2,0,1:T(2,128)(2,1)} %param.5), channel_id=1, replica_groups=mesh['groups'=2,'blk'=4,'head'=4] {'blk'}, dimensions={1}, use_global_device_ids=true | all-gather | bytes 40960 | tf_op jit(solution)/shard_map/all_gather | solution.py:25
  15.8 0.1 slice_reduce_fusion.3
  15.9 0.1 broadcast_compare_fusion.1
  16.0 1.1 %select_reduce_fusion.3 = (f32[4,8]{1,0:T(4,128)S(1)}, f32[4,8,512]{2,1,0:T(8,128)S(1)}) fusion(pred[4,512]{1,0:T(4,128)(4,1)S(1)} %get-tuple-element.13, bf16[2,512,256]{2,1,0:T(8,128)(2,1)} %param.6, bf16[1,4,8,128]{3,1,2,0:T(4,128)(2,1)S(1)} %bitcast.152), kind=kOutput, calls=%fused_computation.36 | convolution fusion | flops 4243424 | bytes 206976 | tf_op jit(solution)/shard_map/ngd,cd->ngc/dot_general | solution.py:51
  17.2 1.1 %select_reduce_fusion.1 = (f32[4,8]{1,0:T(4,128)S(1)}, f32[4,8,512]{2,1,0:T(8,128)S(1)}) fusion(pred[4,512]{1,0:T(4,128)(4,1)S(1)} %get-tuple-element.14, bf16[2,512,256]{2,1,0:T(8,128)(2,1)} %param.6, bf16[1,4,8,128]{3,1,2,0:T(4,128)(2,1)S(1)} %bitcast.151), kind=kOutput, calls=%fused_computation.32 | convolution fusion | flops 4243424 | bytes 206976 | tf_op jit(solution)/shard_map/ngd,cd->ngc/dot_general | solution.py:51
  18.3 1.1 %fusion.19 = (f32[4,8]{1,0:T(4,128)S(1)}, f32[4,8]{1,0:T(4,128)S(1)}, f32[4,8,512]{2,1,0:T(8,128)S(1)}) fusion(f32[4,8,512]{2,1,0:T(8,128)S(1)} %get-tuple-element.21, f32[4,8]{1,0:T(4,128)S(1)} %get-tuple-element.20, pred[4,512]{1,0:T(4,128)(4,1)S(1)} %get-tuple-element.13, bf16[2,512,256]{2,1,0:T(8,128)(2,1)} %param.6, ...), kind=kOutput, calls=%fused_computation.37 | convolution fusion | flops 4292544 | bytes 272768 | tf_op jit(solution)/shard_map/ngd,cd->ngc/dot_general | solution.py:51
  19.4 1.1 %fusion.23 = (f32[4,8]{1,0:T(4,128)S(1)}, f32[4,8]{1,0:T(4,128)S(1)}, f32[4,8,512]{2,1,0:T(8,128)S(1)}) fusion(f32[4,8,512]{2,1,0:T(8,128)S(1)} %get-tuple-element.18, f32[4,8]{1,0:T(4,128)S(1)} %get-tuple-element.17, pred[4,512]{1,0:T(4,128)(4,1)S(1)} %get-tuple-element.14, bf16[2,512,256]{2,1,0:T(8,128)(2,1)} %param.6, ...), kind=kOutput, calls=%fused_computation.41 | convolution fusion | flops 4292544 | bytes 272768 | tf_op jit(solution)/shard_map/ngd,cd->ngc/dot_general | solution.py:51
  20.6 0.1 maximum_bitcast_fusion.3
  20.7 0.6 copy.16
  21.3 4.6 %all-to-all-start.1 = ((f32[1,2,4,16]{3,1,0,2:T(2,128)}), f32[1,2,4,16]{3,1,0,2:T(2,128)S(1)}, u32[]{:S(2)}, u32[]{:S(2)}) async-start(f32[1,2,4,16]{3,1,0,2:T(2,128)} %copy.16), calls=%async_computation.1 | async-start | bytes 8192 | tf_op jit(solution)/shard_map/all_to_all | solution.py:75
  25.9 1.1 %convolution_bitcast_fusion.3 = f32[1,4,8,128]{3,2,1,0:T(8,128)S(1)} fusion(bf16[2,512,256]{2,1,0:T(8,128)(2,1)} %param.7, f32[4,8,512]{2,1,0:T(8,128)S(1)} %get-tuple-element.21, f32[4,8]{1,0:T(4,128)S(1)} %get-tuple-element.20, pred[4,512]{1,0:T(4,128)(4,1)S(1)} %get-tuple-element.13), kind=kOutput, calls=%fused_computation.9 | convolution fusion | flops 4243456 | bytes 215168 | tf_op jit(solution)/shard_map/ngc,cd->ngd/dot_general | solution.py:60
  27.0 1.1 %convolution_bitcast_fusion.1 = f32[1,4,8,128]{3,2,1,0:T(8,128)S(1)} fusion(bf16[2,512,256]{2,1,0:T(8,128)(2,1)} %param.7, f32[4,8,512]{2,1,0:T(8,128)S(1)} %get-tuple-element.18, f32[4,8]{1,0:T(4,128)S(1)} %get-tuple-element.17, pred[4,512]{1,0:T(4,128)(4,1)S(1)} %get-tuple-element.14), kind=kOutput, calls=%fused_computation.7 | convolution fusion | flops 4243456 | bytes 215168 | tf_op jit(solution)/shard_map/ngc,cd->ngd/dot_general | solution.py:60
  28.1 1.1 %convolution_bitcast_fusion.2 = f32[1,4,8,128]{3,2,1,0:T(8,128)S(1)} fusion(bf16[2,512,256]{2,1,0:T(8,128)(2,1)} %param.7, f32[4,8,512]{2,1,0:T(8,128)S(1)} %get-tuple-element.22, f32[4,8]{1,0:T(4,128)S(1)} %get-tuple-element.10, pred[4,512]{1,0:T(4,128)(4,1)S(1)} %get-tuple-element.13), kind=kOutput, calls=%fused_computation.8 | convolution fusion | flops 4243456 | bytes 215168 | tf_op jit(solution)/shard_map/ngc,cd->ngd/dot_general | solution.py:60
  29.2 0.2 fusion.21
  29.4 1.1 %convolution_bitcast_fusion = f32[1,4,8,128]{3,2,1,0:T(8,128)S(1)} fusion(bf16[2,512,256]{2,1,0:T(8,128)(2,1)} %param.7, f32[4,8,512]{2,1,0:T(8,128)S(1)} %get-tuple-element.19, f32[4,8]{1,0:T(4,128)S(1)} %get-tuple-element.12, pred[4,512]{1,0:T(4,128)(4,1)S(1)} %get-tuple-element.14), kind=kOutput, calls=%fused_computation.6 | convolution fusion | flops 4243456 | bytes 215168 | tf_op jit(solution)/shard_map/ngc,cd->ngd/dot_general | solution.py:60
  30.7 0.1 maximum_bitcast_fusion.5
  30.8 0.1 maximum_bitcast_fusion.6
  30.8 0.7 maximum_bitcast_fusion
  31.5 0.6 copy.20
  32.1 1.2 %dynamic-slice = u32[1]{0:T(128)} dynamic-slice(u32[32]{0:T(128)} %constant.21, u32[]{:T(128)S(6)} %add.33), dynamic_slice_sizes={1} | dynamic-slice | bytes 12
  33.4 0.0 all-to-all-done.1
  33.4 5.1 %all-to-all-start.2 = ((f32[1,2,4,16]{3,1,0,2:T(2,128)}), f32[1,2,4,16]{3,1,0,2:T(2,128)S(1)}, u32[]{:S(2)}, u32[]{:S(2)}) async-start(f32[1,2,4,16]{3,1,0,2:T(2,128)} %copy.20), calls=%async_computation.2 | async-start | bytes 8192 | tf_op jit(solution)/shard_map/all_to_all | solution.py:76
  38.5 5.5 %all-to-all-done.2 = f32[1,2,4,16]{3,1,0,2:T(2,128)S(1)} async-done(((f32[1,2,4,16]{3,1,0,2:T(2,128)}), f32[1,2,4,16]{3,1,0,2:T(2,128)S(1)}, u32[]{:S(2)}, u32[]{:S(2)}) %all-to-all-start.2) | async-done | bytes 544 | tf_op jit(solution)/shard_map/all_to_all | solution.py:76
  44.0 3.3 %all-to-all-start = ((f32[1,2,4,2048]{3,1,0,2:T(2,128)}), f32[1,2,4,2048]{3,1,0,2:T(2,128)S(1)}, u32[]{:S(2)}, u32[]{:S(2)}) async-start(f32[1,2,4,2048]{3,1,0,2:T(2,128)} %maximum_bitcast_fusion), calls=%async_computation | async-start | bytes 131072 | tf_op jit(solution)/shard_map/all_to_all | solution.py:74
  47.4 0.1 div.19
  47.4 0.1 mul.44
  47.6 5.5 %all-to-all-done = f32[1,2,4,2048]{3,1,0,2:T(2,128)S(1)} async-done(((f32[1,2,4,2048]{3,1,0,2:T(2,128)}), f32[1,2,4,2048]{3,1,0,2:T(2,128)S(1)}, u32[]{:S(2)}, u32[]{:S(2)}) %all-to-all-start) | async-done | bytes 65568 | tf_op jit(solution)/shard_map/all_to_all | solution.py:74
  53.1 13.1 %all_gather.7 = bf16[2,4,2048]{2,0,1:T(2,128)(2,1)S(1)} all-gather(bf16[2,1,2048]{2,0,1:T(2,128)(2,1)S(1)} %fusion.43), channel_id=1, replica_groups=mesh['groups'=2,'blk'=4,'head'=4] {'blk'}, dimensions={1}, use_global_device_ids=true | all-gather | bytes 40960 | tf_op jit(solution)/shard_map/all_gather | solution.py:91
  66.2 4.7 %fusion = f32[2,4,2048]{2,0,1:T(2,128)S(1)} fusion(bf16[2,4,2048]{2,0,1:T(2,128)(2,1)S(1)} %all_gather.7, bf16[2048,2048]{1,0:T(8,128)(2,1)} %param.8), kind=kOutput, calls=%fused_computation | convolution fusion | flops 67108864 | bytes 8486912 | tf_op jit(solution)/shard_map/rnc,cd->rnd/dot_general | solution.py:89
  71.0 10.7 %all-reduce = bf16[2,4,2048]{2,0,1:T(2,128)(2,1)S(1)} all-reduce(f32[2,4,2048]{2,0,1:T(2,128)S(1)} %fusion), channel_id=2, replica_groups=mesh['groups'=2,'blk'=4,'head'=4] {'head'}, use_global_device_ids=true, to_apply=%region_11.12.clone | all-reduce | flops 16384 | bytes 98304
  81.6 1.2 %dynamic-slice_convert_fusion = bf16[2,1,2048]{2,0,1:T(2,128)(2,1)} fusion(bf16[2,4,2048]{2,0,1:T(2,128)(2,1)S(1)} %all-reduce, u32[]{:T(128)} %bitcast.39), kind=kLoop, calls=%fused_computation.67 | loop fusion | bytes 16388 | tf_op jit(solution)/shard_map/convert_element_type | solution.py:95
  (21 shorter events, 0.3 us)
Async XLA Ops:
  21.3 12.1 %all-to-all-start.1 = ((f32[1,2,4,16]{3,1,0,2:T(2,128)}), f32[1,2,4,16]{3,1,0,2:T(2,128)S(1)}, u32[]{:S(2)}, u32[]{:S(2)}) async-start(f32[1,2,4,16]{3,1,0,2:T(2,128)} %copy.16), calls=%async_computation.1 | async-start | bytes 8192 | tf_op jit(solution)/shard_map/all_to_all | solution.py:75
  33.4 10.7 %all-to-all-start.2 = ((f32[1,2,4,16]{3,1,0,2:T(2,128)}), f32[1,2,4,16]{3,1,0,2:T(2,128)S(1)}, u32[]{:S(2)}, u32[]{:S(2)}) async-start(f32[1,2,4,16]{3,1,0,2:T(2,128)} %copy.20), calls=%async_computation.2 | async-start | bytes 8192 | tf_op jit(solution)/shard_map/all_to_all | solution.py:76
  44.0 9.0 %all-to-all-start = ((f32[1,2,4,2048]{3,1,0,2:T(2,128)}), f32[1,2,4,2048]{3,1,0,2:T(2,128)S(1)}, u32[]{:S(2)}, u32[]{:S(2)}) async-start(f32[1,2,4,2048]{3,1,0,2:T(2,128)} %maximum_bitcast_fusion), calls=%async_computation | async-start | bytes 131072 | tf_op jit(solution)/shard_map/all_to_all | solution.py:74
where the time goes:
time: 83.4 us; the launch traced here: 82.9 us
  blocking collectives  38.8 us (47%)
  matrix products  13.7 us (16%)
  starting transfers between devices  13 us (16%)
  waiting for transfers between devices  11 us (13%)
  local copies, waits for them, and re-layouts  4.11 us (5%)
  other arithmetic  2.04 us (2%)
    all_gather x1, blocking collectives, body(): piece = lax.all_gather(queries, 'blk', axis=1, tiled=True)  15 us
    all_gather x1, blocking collectives, body(): lax.all_gather(own_attention, 'blk', axis=1, tiled=True)  13.1 us
    unnamed x1, blocking collectives  10.7 us
    all_to_all x1, waiting for transfers between devices, body(): lax.all_to_all(new_totals[None], 'blk', split_axis=2, concat_axis=0, tile...  5.54 us
    all_to_all x1, waiting for transfers between devices, body(): lax.all_to_all(new_sums[None], 'blk', split_axis=2, concat_axis=0, tiled=...  5.46 us
    all_to_all x1, starting transfers between devices, body(): lax.all_to_all(new_totals[None], 'blk', split_axis=2, concat_axis=0, tile...  5.09 us
    dot_general x1, matrix products, body(): jnp.einsum('rnc,cd->rnd', lax.all_gather(own_attention, 'blk', axis=1, ti...  4.71 us
    all_to_all x1, starting transfers between devices, body(): lax.all_to_all(new_maxima[None], 'blk', split_axis=2, concat_axis=0, tile...  4.63 us
  transfers between devices with their start and end apart: 3, of which 2 were waited for; matrix products, arithmetic and copies ran while one was open for 9% of the time, Pallas kernels for 0%

commit v1 on v0

--- a/solution.py
+++ b/solution.py
@@ -1,8 +1,11 @@
+import functools
 import math
 
 import jax
 import jax.numpy as jnp
 from jax import lax
+from jax.experimental import pallas as pl
+from jax.experimental.pallas import tpu as pltpu
 from jax.sharding import PartitionSpec as P
 
 REQUEST_COUNT = 2
@@ -12,6 +15,273 @@
 
 
 masked_fill_value = -1e30
+
+
+MESH = pl.DeviceIdType.MESH
+COLUMN_CHUNKS = 4
+
+
+def fused_kernel(
+    dims,
+    lengths_ref,
+    queries_ref,
+    keys_hbm,
+    values_hbm,
+    weight_hbm,
+    out_ref,
+    query_slots,
+    keys_ref,
+    values_ref,
+    weight_ref,
+    sum_slots,
+    stat_slots,
+    acc_ref,
+    terms_ref,
+    term_slots,
+    local_sem,
+    weight_sem,
+    query_send,
+    query_recv,
+    sum_send,
+    sum_recv,
+    stat_send,
+    stat_recv,
+    term_send,
+    term_recv,
+):
+    n_blk, n_head, requests, span, local_heads, group_width = dims
+    my_blk = lax.axis_index("blk")
+    my_head = lax.axis_index("head")
+    rows = n_blk * requests
+    stack = group_width * rows
+    depth = group_width * HEAD_DIMENSION
+    columns = weight_ref.shape[1]
+    width = columns // COLUMN_CHUNKS
+
+    key_copy = pltpu.make_async_copy(keys_hbm, keys_ref, local_sem.at[0])
+    value_copy = pltpu.make_async_copy(values_hbm, values_ref, local_sem.at[1])
+    key_copy.start()
+    value_copy.start()
+    weight_copies = []
+    for kv_head in range(local_heads):
+        part = pl.ds(kv_head * depth, depth)
+        weight_copies.append(
+            pltpu.make_async_copy(
+                weight_hbm.at[part], weight_ref.at[part], weight_sem.at[kv_head]
+            )
+        )
+        weight_copies[-1].start()
+
+    barrier = pltpu.get_barrier_semaphore()
+    for step in range(1, n_blk):
+        peer = lax.rem(my_blk + step, n_blk)
+        pl.semaphore_signal(barrier, inc=1, device_id={"blk": peer}, device_id_type=MESH)
+    for step in range(1, n_head):
+        peer = lax.rem(my_head + step, n_head)
+        pl.semaphore_signal(barrier, inc=1, device_id={"head": peer}, device_id_type=MESH)
+    pl.semaphore_wait(barrier, n_blk + n_head - 2)
+
+    query_copies = []
+    for step in range(1, n_blk):
+        copy = pltpu.make_async_remote_copy(
+            src_ref=queries_ref,
+            dst_ref=query_slots.at[my_blk],
+            send_sem=query_send.at[step],
+            recv_sem=query_recv.at[step],
+            device_id={"blk": lax.rem(my_blk + step, n_blk)},
+            device_id_type=MESH,
+        )
+        copy.start()
+        query_copies.append(copy)
+    query_slots[my_blk] = queries_ref[...]
+
+    row = lax.broadcasted_iota(jnp.int32, (rows, requests * span), 0)
+    column = lax.broadcasted_iota(jnp.int32, (rows, requests * span), 1)
+    token, row_request = row // requests, row % requests
+    position = my_blk * span + column % span
+    visible = jnp.zeros((rows, requests * span), jnp.bool_)
+    for request in range(requests):
+        here = (column // span == request) & (row_request == request)
+        seen = position <= lengths_ref[request] - n_blk + token
+        visible = visible | (here & seen)
+    visible = visible[None]
+    score_scale = 1.0 / math.sqrt(HEAD_DIMENSION)
+    lane = lax.broadcasted_iota(jnp.int32, (stack, 128), 1)
+    diagonal = lane == lax.broadcasted_iota(jnp.int32, (stack, 128), 0)
+
+    for copy in query_copies:
+        copy.wait()
+    gathered = jnp.concatenate(
+        [query_slots[b].astype(jnp.float32) for b in range(n_blk)], axis=0
+    )
+    key_copy.wait()
+    value_copy.wait()
+
+    partial_copies = []
+    for kv_head in range(local_heads):
+        entries = pl.ds(kv_head * HEAD_DIMENSION, HEAD_DIMENSION)
+        block_query = jnp.concatenate(
+            [
+                gathered[:, h * HEAD_DIMENSION : (h + 1) * HEAD_DIMENSION]
+                for h in range(kv_head * group_width, (kv_head + 1) * group_width)
+            ],
+            axis=0,
+        ).astype(jnp.bfloat16)
+        scores = lax.dot_general(
+            block_query,
+            keys_ref[:, entries],
+            (((1,), (1,)), ((), ())),
+            preferred_element_type=jnp.float32,
+        )
+        scores = (scores * score_scale).reshape(group_width, rows, requests * span)
+        block_max = jnp.max(
+            jnp.where(visible, scores, masked_fill_value), axis=-1, keepdims=True
+        )
+        weights = jnp.where(visible, jnp.exp(scores - block_max), 0.0)
+        total = jnp.sum(weights, axis=-1, keepdims=True)
+        weighted = jnp.dot(
+            weights.reshape(stack, requests * span).astype(jnp.bfloat16),
+            values_ref[:, entries],
+            preferred_element_type=jnp.float32,
+        )
+        sum_slots[kv_head, my_blk] = weighted.astype(sum_slots.dtype)
+        stats = [
+            jnp.sum(jnp.where(diagonal, x.reshape(stack, 1), 0.0), axis=0, keepdims=True)
+            for x in (block_max, total)
+        ]
+        stat_slots[kv_head, my_blk] = jnp.concatenate(
+            stats + [jnp.zeros((6, 128), jnp.float32)], axis=0
+        )
+        copies = []
+        for step in range(1, n_blk):
+            peer = lax.rem(my_blk + step, n_blk)
+            for slots, send, recv in (
+                (stat_slots, stat_send, stat_recv),
+                (sum_slots, sum_send, sum_recv),
+            ):
+                copy = pltpu.make_async_remote_copy(
+                    src_ref=slots.at[kv_head, my_blk],
+                    dst_ref=slots.at[kv_head, my_blk],
+                    send_sem=send.at[kv_head, step],
+                    recv_sem=recv.at[kv_head, step],
+                    device_id={"blk": peer},
+                    device_id_type=MESH,
+                )
+                copy.start()
+                copies.append(copy)
+        partial_copies.append(copies)
+
+    term_copies = []
+    for kv_head in range(local_heads):
+        for copy in partial_copies[kv_head]:
+            copy.wait()
+        maxima = [stat_slots[kv_head, b, 0:1, :] for b in range(n_blk)]
+        totals = [stat_slots[kv_head, b, 1:2, :] for b in range(n_blk)]
+        top = functools.reduce(jnp.maximum, maxima)
+        factors = [jnp.exp(x - top) for x in maxima]
+        overall = sum(f * x for f, x in zip(factors, totals))
+        overall = jnp.where(lane[0:1] < stack, overall, 1.0)
+        merged = jnp.zeros((stack, HEAD_DIMENSION), jnp.float32)
+        for b in range(n_blk):
+            share = jnp.sum(
+                jnp.where(diagonal, factors[b] / overall, 0.0), axis=1, keepdims=True
+            )
+            merged = merged + sum_slots[kv_head, b].astype(jnp.float32) * share
+        attention = jnp.concatenate(
+            [merged[g * rows : (g + 1) * rows] for g in range(group_width)], axis=1
+        ).astype(jnp.bfloat16)
+        weight_copies[kv_head].wait()
+        part = pl.ds(kv_head * depth, depth)
+        for chunk in range(COLUMN_CHUNKS):
+            where = pl.ds(chunk * width, width)
+            term = jnp.dot(
+                attention, weight_ref[part, where], preferred_element_type=jnp.float32
+            )
+            if kv_head > 0:
+                term = term + acc_ref[:, where]
+            if kv_head < local_heads - 1:
+                acc_ref[:, where] = term
+                continue
+            for h in range(n_head):
+                terms_ref[chunk, h] = term[h * requests : (h + 1) * requests]
+            for step in range(1, n_head):
+                peer = lax.rem(my_head + step, n_head)
+                copy = pltpu.make_async_remote_copy(
+                    src_ref=terms_ref.at[chunk, peer],
+                    dst_ref=term_slots.at[chunk, step],
+                    send_sem=term_send.at[chunk, step],
+                    recv_sem=term_recv.at[chunk, step],
+                    device_id={"head": peer},
+                    device_id_type=MESH,
+                )
+                copy.start()
+                term_copies.append(copy)
+
+    for chunk in range(COLUMN_CHUNKS):
+        result = terms_ref[chunk, my_head]
+        for step in range(1, n_head):
+            term_copies[chunk * (n_head - 1) + step - 1].wait()
+            result = result + term_slots[chunk, step]
+        out_ref[:, pl.ds(chunk * width, width)] = result.astype(out_ref.dtype)
+
+
+def fused(queries, stored_cache_keys, stored_cache_values, out_weight, lengths):
+    n_blk, n_head = lax.axis_size("blk"), lax.axis_size("head")
+    requests, span, kv_width = stored_cache_keys.shape
+    group_width = QUERY_HEAD_COUNT // KEY_VALUE_HEADS
+    local_heads = kv_width // HEAD_DIMENSION
+    inputs, columns = out_weight.shape
+    rows = requests * n_blk
+    stack = group_width * rows
+    width = columns // COLUMN_CHUNKS
+    dims = (n_blk, n_head, requests, span, local_heads, group_width)
+    vmem = pl.BlockSpec(memory_space=pltpu.VMEM)
+    hbm = pl.BlockSpec(memory_space=pl.ANY)
+    out = pl.pallas_call(
+        functools.partial(fused_kernel, dims),
+        out_shape=jax.ShapeDtypeStruct((requests, columns), jnp.bfloat16),
+        in_specs=[pl.BlockSpec(memory_space=pltpu.SMEM), vmem, hbm, hbm, hbm],
+        out_specs=vmem,
+        scratch_shapes=[
+            pltpu.VMEM((n_blk, requests, inputs), jnp.bfloat16),
+            pltpu.VMEM((requests * span, kv_width), jnp.bfloat16),
+            pltpu.VMEM((requests * span, kv_width), jnp.bfloat16),
+            pltpu.VMEM((inputs, columns), jnp.bfloat16),
+            pltpu.VMEM((local_heads, n_blk, stack, HEAD_DIMENSION), jnp.bfloat16),
+            pltpu.VMEM((local_heads, n_blk, 8, 128), jnp.float32),
+            pltpu.VMEM((rows, columns), jnp.float32),
+            pltpu.VMEM((COLUMN_CHUNKS, n_head, requests, width), jnp.float32),
+            pltpu.VMEM((COLUMN_CHUNKS, n_head, requests, width), jnp.float32),
+            pltpu.SemaphoreType.DMA((2,)),
+            pltpu.SemaphoreType.DMA((local_heads,)),
+            pltpu.SemaphoreType.DMA((n_blk,)),
+            pltpu.SemaphoreType.DMA((n_blk,)),
+            pltpu.SemaphoreType.DMA((local_heads, n_blk)),
+            pltpu.SemaphoreType.DMA((local_heads, n_blk)),
+            pltpu.SemaphoreType.DMA((local_heads, n_blk)),
+            pltpu.SemaphoreType.DMA((local_heads, n_blk)),
+            pltpu.SemaphoreType.DMA((COLUMN_CHUNKS, n_head)),
+            pltpu.SemaphoreType.DMA((COLUMN_CHUNKS, n_head)),
+        ],
+        compiler_params=pltpu.CompilerParams(collective_id=0, has_side_effects=True),
+    )(
+        lengths,
+        queries.reshape(requests, inputs),
+        stored_cache_keys.reshape(requests * span, kv_width),
+        stored_cache_values.reshape(requests * span, kv_width),
+        out_weight,
+    )
+    return out.reshape(requests, 1, columns)
+
+
+def layer(queries, stored_cache_keys, *others):
+    tokens = queries.shape[1] * lax.axis_size("blk")
+    fits = (
+        queries.shape[1] == 1
+        and tokens == lax.axis_size("head")
+        and tokens * queries.shape[0] == 8
+    )
+    return (fused if fits else body)(queries, stored_cache_keys, *others)
 
 
 def body(queries, stored_cache_keys, stored_cache_values, out_weight, lengths):
@@ -104,5 +374,5 @@
         P("groups"),
     )
     return jax.shard_map(
-        body, mesh=mesh, in_specs=placed, out_specs=P("groups", "head", "blk"), check_vma=False
-    )
+        layer, mesh=mesh, in_specs=placed, out_specs=P("groups", "head", "blk"), check_vma=False
+    )

time: 83.4 us -> 21.5 us (0.26)
  blocking collectives: 38.8 us -> 0 us
  Pallas kernels: 0 us -> 19.9 us
  matrix products: 13.7 us -> 0 us
  starting transfers between devices: 13 us -> 0 us
  waiting for transfers between devices: 11 us -> 0 us
  local copies, waits for them, and re-layouts: 4.11 us -> 1.3 us
  other arithmetic: 2.04 us -> 0 us
    all_gather x2 -> x0, blocking collectives: 28.2 us -> none  [the longest x1 15 us: body(): piece = lax.all_gather(queries, 'blk', axis=1, tiled=True)]
    pallas_call x0 -> x1, Pallas kernels: none -> 19.9 us  [fused(): pl.pallas_call(functools.partial(fused_kernel, dims), out_shape=jax.Shape...]
    dot_general x9 -> x0, matrix products: 13.7 us -> none  [the longest x1 4.71 us: body(): jnp.einsum('rnc,cd->rnd', lax.all_gather(own_attention, 'blk', axis=1, ti...]
    all_to_all x3 -> x0, starting transfers between devices: 13 us -> none  [the longest x1 5.09 us: body(): lax.all_to_all(new_totals[None], 'blk', split_axis=2, concat_axis=0, tile...]
    all_to_all x3 -> x0, waiting for transfers between devices: 11 us -> none  [the longest x1 5.54 us: body(): lax.all_to_all(new_totals[None], 'blk', split_axis=2, concat_axis=0, tile...]
    unnamed x1 -> x0, blocking collectives: 10.7 us -> none
    convert_element_type x1 -> x0, local copies, waits for them, and re-layouts: 1.23 us -> none  [body(): lax.psum_scatter(terms, 'head', scatter_dimension=1, tiled=True)]
    broadcast_in_dim x2 -> x0, local copies, waits for them, and re-layouts: 1.2 us -> none  [the longest x1 0.6 us: body(): new_maxima[None]]
  transfers between devices with their start and end apart: 3 -> 0, of which waited for: 2 -> 0; matrix products, arithmetic and copies ran while one was open for 9% -> 0% of each run, Pallas kernels for 0% -> 0%
where the time goes in v1:
time: 21.5 us; the launch traced here: 21.2 us
  Pallas kernels  19.9 us (93%)
  local copies, waits for them, and re-layouts  1.3 us (6%)
    pallas_call x1, Pallas kernels, fused(): pl.pallas_call(functools.partial(fused_kernel, dims), out_shape=jax.Shape...  19.9 us
    unnamed x1, local copies, waits for them, and re-layouts  1.3 us

profile of v1, /device:TPU:0, one launch (start us, length us, event | category | flops | bytes accessed | tf_op | source)
XLA Modules:
  0.0 21.2 jit_solution(13533516962104321127)
XLA Ops:
  0.0 19.9 %shard_map.55 = bf16[2,2048]{1,0:T(2,128)(2,1)} custom-call(s32[2]{0:T(128)} %lengths_ref.1, bf16[2,2048]{1,0:T(2,128)(2,1)} %bitcast.7, bf16[1024,256]{1,0:T(8,128)(2,1)} %bitcast.4, bf16[1024,256]{1,0:T(8,128)(2,1)} %bitcast.5, bf16[2048,2048]{1,0:T(8,128)(2,1)} %weight_hbm.1), custom_call_target="tpu_custom_call" | custom-call | tf_op jit(solution)/shard_map/pallas_call | solution.py:240
  19.9 1.3 %copy.7 = bf16[2,1,2048]{2,0,1:T(2,128)(2,1)} copy(bf16[2,1,2048]{2,0,1:T(2,128)(2,1)} %bitcast.6) | data formatting | bytes 16384

commit v2 on v1

--- a/solution.py
+++ b/solution.py
@@ -18,17 +18,19 @@
 
 
 MESH = pl.DeviceIdType.MESH
-COLUMN_CHUNKS = 4
+COLUMN_CHUNKS = 1
+LANES = 128
 
 
 def fused_kernel(
     dims,
-    lengths_ref,
-    queries_ref,
+    lengths_hbm,
+    queries_hbm,
     keys_hbm,
     values_hbm,
     weight_hbm,
     out_ref,
+    lengths_ref,
     query_slots,
     keys_ref,
     values_ref,
@@ -58,6 +60,19 @@
     columns = weight_ref.shape[1]
     width = columns // COLUMN_CHUNKS
 
+    barrier = pltpu.get_barrier_semaphore()
+    for step in range(1, n_blk):
+        peer = lax.rem(my_blk + step, n_blk)
+        pl.semaphore_signal(barrier, inc=1, device_id={"blk": peer}, device_id_type=MESH)
+    for step in range(1, n_head):
+        peer = lax.rem(my_head + step, n_head)
+        pl.semaphore_signal(barrier, inc=1, device_id={"head": peer}, device_id_type=MESH)
+    query_copy = pltpu.make_async_copy(
+        queries_hbm, query_slots.at[my_blk], local_sem.at[2]
+    )
+    query_copy.start()
+    length_copy = pltpu.make_async_copy(lengths_hbm, lengths_ref, local_sem.at[3])
+    length_copy.start()
     key_copy = pltpu.make_async_copy(keys_hbm, keys_ref, local_sem.at[0])
     value_copy = pltpu.make_async_copy(values_hbm, values_ref, local_sem.at[1])
     key_copy.start()
@@ -72,19 +87,13 @@
         )
         weight_copies[-1].start()
 
-    barrier = pltpu.get_barrier_semaphore()
-    for step in range(1, n_blk):
-        peer = lax.rem(my_blk + step, n_blk)
-        pl.semaphore_signal(barrier, inc=1, device_id={"blk": peer}, device_id_type=MESH)
-    for step in range(1, n_head):
-        peer = lax.rem(my_head + step, n_head)
-        pl.semaphore_signal(barrier, inc=1, device_id={"head": peer}, device_id_type=MESH)
+    query_copy.wait()
     pl.semaphore_wait(barrier, n_blk + n_head - 2)
 
     query_copies = []
     for step in range(1, n_blk):
         copy = pltpu.make_async_remote_copy(
-            src_ref=queries_ref,
+            src_ref=query_slots.at[my_blk],
             dst_ref=query_slots.at[my_blk],
             send_sem=query_send.at[step],
             recv_sem=query_recv.at[step],
@@ -93,7 +102,7 @@
         )
         copy.start()
         query_copies.append(copy)
-    query_slots[my_blk] = queries_ref[...]
+    length_copy.wait()
 
     row = lax.broadcasted_iota(jnp.int32, (rows, requests * span), 0)
     column = lax.broadcasted_iota(jnp.int32, (rows, requests * span), 1)
@@ -106,8 +115,9 @@
         visible = visible | (here & seen)
     visible = visible[None]
     score_scale = 1.0 / math.sqrt(HEAD_DIMENSION)
-    lane = lax.broadcasted_iota(jnp.int32, (stack, 128), 1)
-    diagonal = lane == lax.broadcasted_iota(jnp.int32, (stack, 128), 0)
+    lane = lax.broadcasted_iota(jnp.int32, (stack, LANES), 1)
+    own_lane = lax.broadcasted_iota(jnp.int32, (stack, LANES), 0)
+    max_place, total_place = lane == own_lane, lane == own_lane + LANES // 2
 
     for copy in query_copies:
         copy.wait()
@@ -145,13 +155,12 @@
             preferred_element_type=jnp.float32,
         )
         sum_slots[kv_head, my_blk] = weighted.astype(sum_slots.dtype)
-        stats = [
-            jnp.sum(jnp.where(diagonal, x.reshape(stack, 1), 0.0), axis=0, keepdims=True)
-            for x in (block_max, total)
-        ]
-        stat_slots[kv_head, my_blk] = jnp.concatenate(
-            stats + [jnp.zeros((6, 128), jnp.float32)], axis=0
-        )
+        stats = jnp.where(
+            max_place,
+            block_max.reshape(stack, 1),
+            jnp.where(total_place, total.reshape(stack, 1), 0.0),
+        )
+        stat_slots[kv_head, my_blk] = jnp.sum(stats, axis=0, keepdims=True)
         copies = []
         for step in range(1, n_blk):
             peer = lax.rem(my_blk + step, n_blk)
@@ -175,8 +184,8 @@
     for kv_head in range(local_heads):
         for copy in partial_copies[kv_head]:
             copy.wait()
-        maxima = [stat_slots[kv_head, b, 0:1, :] for b in range(n_blk)]
-        totals = [stat_slots[kv_head, b, 1:2, :] for b in range(n_blk)]
+        maxima = [stat_slots[kv_head, b] for b in range(n_blk)]
+        totals = [pltpu.roll(x, LANES // 2, 1) for x in maxima]
         top = functools.reduce(jnp.maximum, maxima)
         factors = [jnp.exp(x - top) for x in maxima]
         overall = sum(f * x for f, x in zip(factors, totals))
@@ -184,7 +193,7 @@
         merged = jnp.zeros((stack, HEAD_DIMENSION), jnp.float32)
         for b in range(n_blk):
             share = jnp.sum(
-                jnp.where(diagonal, factors[b] / overall, 0.0), axis=1, keepdims=True
+                jnp.where(max_place, factors[b] / overall, 0.0), axis=1, keepdims=True
             )
             merged = merged + sum_slots[kv_head, b].astype(jnp.float32) * share
         attention = jnp.concatenate(
@@ -240,19 +249,20 @@
     out = pl.pallas_call(
         functools.partial(fused_kernel, dims),
         out_shape=jax.ShapeDtypeStruct((requests, columns), jnp.bfloat16),
-        in_specs=[pl.BlockSpec(memory_space=pltpu.SMEM), vmem, hbm, hbm, hbm],
+        in_specs=[hbm] * 5,
         out_specs=vmem,
         scratch_shapes=[
+            pltpu.SMEM((requests,), jnp.int32),
             pltpu.VMEM((n_blk, requests, inputs), jnp.bfloat16),
             pltpu.VMEM((requests * span, kv_width), jnp.bfloat16),
             pltpu.VMEM((requests * span, kv_width), jnp.bfloat16),
             pltpu.VMEM((inputs, columns), jnp.bfloat16),
             pltpu.VMEM((local_heads, n_blk, stack, HEAD_DIMENSION), jnp.bfloat16),
-            pltpu.VMEM((local_heads, n_blk, 8, 128), jnp.float32),
+            pltpu.VMEM((local_heads, n_blk, 1, LANES), jnp.float32),
             pltpu.VMEM((rows, columns), jnp.float32),
             pltpu.VMEM((COLUMN_CHUNKS, n_head, requests, width), jnp.float32),
             pltpu.VMEM((COLUMN_CHUNKS, n_head, requests, width), jnp.float32),
-            pltpu.SemaphoreType.DMA((2,)),
+            pltpu.SemaphoreType.DMA((4,)),
             pltpu.SemaphoreType.DMA((local_heads,)),
             pltpu.SemaphoreType.DMA((n_blk,)),
             pltpu.SemaphoreType.DMA((n_blk,)),
@@ -280,6 +290,7 @@
         queries.shape[1] == 1
         and tokens == lax.axis_size("head")
         and tokens * queries.shape[0] == 8
+        and QUERY_HEAD_COUNT // KEY_VALUE_HEADS * 8 == LANES // 2
     )
     return (fused if fits else body)(queries, stored_cache_keys, *others)
 

time: 21.5 us -> 20.4 us (0.949)
  Pallas kernels: 19.9 us -> 18.8 us
    pallas_call x1, Pallas kernels: 19.9 us -> 18.8 us  [fused(): pl.pallas_call(functools.partial(fused_kernel, dims), out_shape=jax.Shape...]
where the time goes in v2:
time: 20.4 us; the launch traced here: 20.2 us
  Pallas kernels  18.8 us (92%)
  local copies, waits for them, and re-layouts  1.3 us (6%)
    pallas_call x1, Pallas kernels, fused(): pl.pallas_call(functools.partial(fused_kernel, dims), out_shape=jax.Shape...  18.8 us
    unnamed x1, local copies, waits for them, and re-layouts  1.3 us

profile of v2, /device:TPU:0, one launch (start us, length us, event | category | flops | bytes accessed | tf_op | source)
XLA Modules:
  0.0 20.2 jit_solution(13462711750921416729)
XLA Ops:
  0.0 18.8 %shard_map.55 = bf16[2,2048]{1,0:T(2,128)(2,1)} custom-call(s32[2]{0:T(128)} %lengths_hbm.1, bf16[2,2048]{1,0:T(2,128)(2,1)} %bitcast.7, bf16[1024,256]{1,0:T(8,128)(2,1)} %bitcast.4, bf16[1024,256]{1,0:T(8,128)(2,1)} %bitcast.5, bf16[2048,2048]{1,0:T(8,128)(2,1)} %weight_hbm.1), custom_call_target="tpu_custom_call" | custom-call | tf_op jit(solution)/shard_map/pallas_call | solution.py:249
  18.9 1.3 %copy.7 = bf16[2,1,2048]{2,0,1:T(2,128)(2,1)} copy(bf16[2,1,2048]{2,0,1:T(2,128)(2,1)} %bitcast.6) | data formatting | bytes 16384

commit v3 on v2

--- a/solution.py
+++ b/solution.py
@@ -29,7 +29,7 @@
     keys_hbm,
     values_hbm,
     weight_hbm,
-    out_ref,
+    parts_hbm,
     lengths_ref,
     query_slots,
     keys_ref,
@@ -39,7 +39,6 @@
     stat_slots,
     acc_ref,
     terms_ref,
-    term_slots,
     local_sem,
     weight_sem,
     query_send,
@@ -90,14 +89,21 @@
     query_copy.wait()
     pl.semaphore_wait(barrier, n_blk + n_head - 2)
 
+    peers = []
+    for k in range(n_blk - 1):
+        down = n_blk - 1 - k
+        down = jnp.where(down <= my_blk, down - 1, down)
+        up = jnp.where(k >= my_blk, k + 1, k)
+        peers.append(jnp.where(my_blk < n_blk // 2, down, up))
+
     query_copies = []
-    for step in range(1, n_blk):
+    for peer in peers:
         copy = pltpu.make_async_remote_copy(
             src_ref=query_slots.at[my_blk],
             dst_ref=query_slots.at[my_blk],
-            send_sem=query_send.at[step],
-            recv_sem=query_recv.at[step],
-            device_id={"blk": lax.rem(my_blk + step, n_blk)},
+            send_sem=query_send.at[peer],
+            recv_sem=query_recv.at[my_blk],
+            device_id={"blk": peer},
             device_id_type=MESH,
         )
         copy.start()
@@ -119,8 +125,10 @@
     own_lane = lax.broadcasted_iota(jnp.int32, (stack, LANES), 0)
     max_place, total_place = lane == own_lane, lane == own_lane + LANES // 2
 
-    for copy in query_copies:
-        copy.wait()
+    for peer, copy in zip(peers, query_copies):
+        pltpu.make_async_copy(
+            query_slots.at[peer], query_slots.at[peer], query_recv.at[peer]
+        ).wait()
     gathered = jnp.concatenate(
         [query_slots[b].astype(jnp.float32) for b in range(n_blk)], axis=0
     )
@@ -162,8 +170,7 @@
         )
         stat_slots[kv_head, my_blk] = jnp.sum(stats, axis=0, keepdims=True)
         copies = []
-        for step in range(1, n_blk):
-            peer = lax.rem(my_blk + step, n_blk)
+        for peer in peers:
             for slots, send, recv in (
                 (stat_slots, stat_send, stat_recv),
                 (sum_slots, sum_send, sum_recv),
@@ -171,8 +178,8 @@
                 copy = pltpu.make_async_remote_copy(
                     src_ref=slots.at[kv_head, my_blk],
                     dst_ref=slots.at[kv_head, my_blk],
-                    send_sem=send.at[kv_head, step],
-                    recv_sem=recv.at[kv_head, step],
+                    send_sem=send.at[kv_head, peer],
+                    recv_sem=recv.at[kv_head, my_blk],
                     device_id={"blk": peer},
                     device_id_type=MESH,
                 )
@@ -182,8 +189,10 @@
 
     term_copies = []
     for kv_head in range(local_heads):
-        for copy in partial_copies[kv_head]:
-            copy.wait()
+        for peer in peers:
+            for slots, recv in ((stat_slots, stat_recv), (sum_slots, sum_recv)):
+                here = slots.at[kv_head, peer]
+                pltpu.make_async_copy(here, here, recv.at[kv_head, peer]).wait()
         maxima = [stat_slots[kv_head, b] for b in range(n_blk)]
         totals = [pltpu.roll(x, LANES // 2, 1) for x in maxima]
         top = functools.reduce(jnp.maximum, maxima)
@@ -213,11 +222,18 @@
                 continue
             for h in range(n_head):
                 terms_ref[chunk, h] = term[h * requests : (h + 1) * requests]
+            own_copy = pltpu.make_async_copy(
+                terms_ref.at[chunk, my_head],
+                parts_hbm.at[chunk, my_head],
+                term_send.at[chunk, 0],
+            )
+            own_copy.start()
+            term_copies.append(own_copy)
             for step in range(1, n_head):
                 peer = lax.rem(my_head + step, n_head)
                 copy = pltpu.make_async_remote_copy(
                     src_ref=terms_ref.at[chunk, peer],
-                    dst_ref=term_slots.at[chunk, step],
+                    dst_ref=parts_hbm.at[chunk, my_head],
                     send_sem=term_send.at[chunk, step],
                     recv_sem=term_recv.at[chunk, step],
                     device_id={"head": peer},
@@ -226,12 +242,11 @@
                 copy.start()
                 term_copies.append(copy)
 
-    for chunk in range(COLUMN_CHUNKS):
-        result = terms_ref[chunk, my_head]
-        for step in range(1, n_head):
-            term_copies[chunk * (n_head - 1) + step - 1].wait()
-            result = result + term_slots[chunk, step]
-        out_ref[:, pl.ds(chunk * width, width)] = result.astype(out_ref.dtype)
+    for copy in term_copies:
+        copy.wait()
+    for copies in [query_copies] + partial_copies:
+        for copy in copies:
+            copy.wait_send()
 
 
 def fused(queries, stored_cache_keys, stored_cache_values, out_weight, lengths):
@@ -244,13 +259,14 @@
     stack = group_width * rows
     width = columns // COLUMN_CHUNKS
     dims = (n_blk, n_head, requests, span, local_heads, group_width)
-    vmem = pl.BlockSpec(memory_space=pltpu.VMEM)
     hbm = pl.BlockSpec(memory_space=pl.ANY)
-    out = pl.pallas_call(
+    parts = pl.pallas_call(
         functools.partial(fused_kernel, dims),
-        out_shape=jax.ShapeDtypeStruct((requests, columns), jnp.bfloat16),
+        out_shape=jax.ShapeDtypeStruct(
+            (COLUMN_CHUNKS, n_head, requests, width), jnp.float32
+        ),
         in_specs=[hbm] * 5,
-        out_specs=vmem,
+        out_specs=hbm,
         scratch_shapes=[
             pltpu.SMEM((requests,), jnp.int32),
             pltpu.VMEM((n_blk, requests, inputs), jnp.bfloat16),
@@ -260,7 +276,6 @@
             pltpu.VMEM((local_heads, n_blk, stack, HEAD_DIMENSION), jnp.bfloat16),
             pltpu.VMEM((local_heads, n_blk, 1, LANES), jnp.float32),
             pltpu.VMEM((rows, columns), jnp.float32),
-            pltpu.VMEM((COLUMN_CHUNKS, n_head, requests, width), jnp.float32),
             pltpu.VMEM((COLUMN_CHUNKS, n_head, requests, width), jnp.float32),
             pltpu.SemaphoreType.DMA((4,)),
             pltpu.SemaphoreType.DMA((local_heads,)),
@@ -281,7 +296,8 @@
         stored_cache_values.reshape(requests * span, kv_width),
         out_weight,
     )
-    return out.reshape(requests, 1, columns)
+    summed = jnp.sum(parts, axis=1).astype(jnp.bfloat16)
+    return summed.transpose(1, 0, 2).reshape(requests, 1, columns)
 
 
 def layer(queries, stored_cache_keys, *others):

time: 20.4 us -> 19.9 us (0.975)
  other arithmetic: 0 us -> 1.47 us
  local copies, waits for them, and re-layouts: 1.3 us -> 0 us
  Pallas kernels: 18.8 us -> 18.2 us
    reduce_sum x0 -> x1, other arithmetic: none -> 1.47 us  [fused(): summed = jnp.sum(parts, axis=1).astype(jnp.bfloat16)]
    unnamed x1 -> x0, local copies, waits for them, and re-layouts: 1.3 us -> none
    pallas_call x1, Pallas kernels: 18.8 us -> 18.2 us  [fused(): pl.pallas_call(functools.partial(fused_kernel, dims), out_shape=jax.Shape...]
where the time goes in v3:
time: 19.9 us; the launch traced here: 19.7 us
  Pallas kernels  18.2 us (91%)
  other arithmetic  1.47 us (7%)
    pallas_call x1, Pallas kernels, fused(): pl.pallas_call(functools.partial(fused_kernel, dims), out_shape=jax.Shape...  18.2 us
    reduce_sum x1, other arithmetic, fused(): summed = jnp.sum(parts, axis=1).astype(jnp.bfloat16)  1.47 us

profile of v3, /device:TPU:0, one launch (start us, length us, event | category | flops | bytes accessed | tf_op | source)
XLA Modules:
  0.0 19.7 jit_solution(9457452743201943415)
XLA Ops:
  0.0 18.2 %shard_map.55 = f32[1,4,2,2048]{3,2,1,0:T(2,128)} custom-call(s32[2]{0:T(128)} %lengths_hbm.1, bf16[2,2048]{1,0:T(2,128)(2,1)} %bitcast.8, bf16[1024,256]{1,0:T(8,128)(2,1)} %bitcast.6, bf16[1024,256]{1,0:T(8,128)(2,1)} %bitcast.7, bf16[2048,2048]{1,0:T(8,128)(2,1)} %weight_hbm.1), custom_call_target="tpu_custom_call" | custom-call | tf_op jit(solution)/shard_map/pallas_call | solution.py:263
  18.2 1.5 %reduce_sum.9 = bf16[2,2048]{1,0:T(2,128)(2,1)} reduce(f32[1,4,2,2048]{3,2,1,0:T(2,128)} %shard_map.55, f32[]{:T(128)} %constant.0.clone.1), dimensions={0,1}, to_apply=%region_0.0 | reduce | flops 12288 | bytes 73732 | tf_op jit(solution)/shard_map/reduce_sum | solution.py:299

commit v4 on v3

--- a/solution.py
+++ b/solution.py
@@ -288,13 +288,18 @@
             pltpu.SemaphoreType.DMA((COLUMN_CHUNKS, n_head)),
             pltpu.SemaphoreType.DMA((COLUMN_CHUNKS, n_head)),
         ],
-        compiler_params=pltpu.CompilerParams(collective_id=0, has_side_effects=True),
+        compiler_params=pltpu.CompilerParams(collective_id=0, vmem_limit_bytes=32768 * 1024, has_side_effects=True),
     )(
-        lengths,
-        queries.reshape(requests, inputs),
-        stored_cache_keys.reshape(requests * span, kv_width),
-        stored_cache_values.reshape(requests * span, kv_width),
-        out_weight,
+        *(
+            pltpu.with_memory_space_constraint(x, pltpu.HBM)
+            for x in (
+                lengths,
+                queries.reshape(requests, inputs),
+                stored_cache_keys.reshape(requests * span, kv_width),
+                stored_cache_values.reshape(requests * span, kv_width),
+                out_weight,
+            )
+        )
     )
     summed = jnp.sum(parts, axis=1).astype(jnp.bfloat16)
     return summed.transpose(1, 0, 2).reshape(requests, 1, columns)

time: 19.9 us -> 19 us (0.955)
  other arithmetic: 1.47 us -> 0.63 us
    reduce_sum x1, other arithmetic: 1.47 us -> 0.63 us  [fused(): summed = jnp.sum(parts, axis=1).astype(jnp.bfloat16)]
where the time goes in v4:
time: 19 us; the launch traced here: 18.8 us
  Pallas kernels  18.1 us (95%)
  other arithmetic  0.63 us (3%)
    pallas_call x1, Pallas kernels, fused(): pl.pallas_call(functools.partial(fused_kernel, dims), out_shape=jax.Shape...  18.1 us
    reduce_sum x1, other arithmetic, fused(): summed = jnp.sum(parts, axis=1).astype(jnp.bfloat16)  0.63 us

profile of v4, /device:TPU:0, one launch (start us, length us, event | category | flops | bytes accessed | tf_op | source)
XLA Modules:
  0.0 18.8 jit_solution(9492042179024503529)
XLA Ops:
  0.0 18.1 %shard_map.55 = f32[1,4,2,2048]{3,2,1,0:T(2,128)S(1)} custom-call(s32[2]{0:T(128)} %lengths_hbm.1, bf16[2,2048]{1,0:T(2,128)(2,1)} %bitcast.8, bf16[1024,256]{1,0:T(8,128)(2,1)} %bitcast.6, bf16[1024,256]{1,0:T(8,128)(2,1)} %bitcast.7, bf16[2048,2048]{1,0:T(8,128)(2,1)} %weight_hbm.1), custom_call_target="tpu_custom_call" | custom-call | tf_op jit(solution)/shard_map/pallas_call | solution.py:263
  18.1 0.6 %reduce_sum.9 = bf16[2,2048]{1,0:T(2,128)(2,1)} reduce(f32[1,4,2,2048]{3,2,1,0:T(2,128)S(1)} %shard_map.55, f32[]{:T(128)} %constant.0.clone.1), dimensions={0,1}, to_apply=%region_0.0 | reduce | flops 12288 | bytes 73732 | tf_op jit(solution)/shard_map/reduce_sum | solution.py:304

commit v5 on v4

--- a/solution.py
+++ b/solution.py
@@ -20,6 +20,8 @@
 MESH = pl.DeviceIdType.MESH
 COLUMN_CHUNKS = 1
 LANES = 128
+TILE_ROWS = 16
+PARTS = 3
 
 
 def fused_kernel(
@@ -36,7 +38,6 @@
     values_ref,
     weight_ref,
     sum_slots,
-    stat_slots,
     acc_ref,
     terms_ref,
     local_sem,
@@ -45,8 +46,6 @@
     query_recv,
     sum_send,
     sum_recv,
-    stat_send,
-    stat_recv,
     term_send,
     term_recv,
 ):
@@ -125,15 +124,15 @@
     own_lane = lax.broadcasted_iota(jnp.int32, (stack, LANES), 0)
     max_place, total_place = lane == own_lane, lane == own_lane + LANES // 2
 
-    for peer, copy in zip(peers, query_copies):
+    key_copy.wait()
+    value_copy.wait()
+    for peer in peers:
         pltpu.make_async_copy(
             query_slots.at[peer], query_slots.at[peer], query_recv.at[peer]
         ).wait()
     gathered = jnp.concatenate(
         [query_slots[b].astype(jnp.float32) for b in range(n_blk)], axis=0
     )
-    key_copy.wait()
-    value_copy.wait()
 
     partial_copies = []
     for kv_head in range(local_heads):
@@ -162,38 +161,45 @@
             values_ref[:, entries],
             preferred_element_type=jnp.float32,
         )
-        sum_slots[kv_head, my_blk] = weighted.astype(sum_slots.dtype)
         stats = jnp.where(
             max_place,
             block_max.reshape(stack, 1),
             jnp.where(total_place, total.reshape(stack, 1), 0.0),
         )
-        stat_slots[kv_head, my_blk] = jnp.sum(stats, axis=0, keepdims=True)
+        rest = jnp.sum(stats, axis=0, keepdims=True)
+        parts = []
+        for _ in range(PARTS):
+            parts.append(rest.astype(jnp.bfloat16).astype(jnp.float32))
+            rest = rest - parts[-1]
+        parts.append(jnp.zeros((TILE_ROWS - PARTS, LANES), jnp.float32))
+        sum_slots[kv_head, my_blk] = jnp.concatenate(
+            [weighted] + parts, axis=0
+        ).astype(jnp.bfloat16)
         copies = []
         for peer in peers:
-            for slots, send, recv in (
-                (stat_slots, stat_send, stat_recv),
-                (sum_slots, sum_send, sum_recv),
-            ):
-                copy = pltpu.make_async_remote_copy(
-                    src_ref=slots.at[kv_head, my_blk],
-                    dst_ref=slots.at[kv_head, my_blk],
-                    send_sem=send.at[kv_head, peer],
-                    recv_sem=recv.at[kv_head, my_blk],
-                    device_id={"blk": peer},
-                    device_id_type=MESH,
-                )
-                copy.start()
-                copies.append(copy)
+            copy = pltpu.make_async_remote_copy(
+                src_ref=sum_slots.at[kv_head, my_blk],
+                dst_ref=sum_slots.at[kv_head, my_blk],
+                send_sem=sum_send.at[kv_head, peer],
+                recv_sem=sum_recv.at[kv_head, my_blk],
+                device_id={"blk": peer},
+                device_id_type=MESH,
+            )
+            copy.start()
+            copies.append(copy)
         partial_copies.append(copies)
 
+    for copy in weight_copies:
+        copy.wait()
     term_copies = []
     for kv_head in range(local_heads):
         for peer in peers:
-            for slots, recv in ((stat_slots, stat_recv), (sum_slots, sum_recv)):
-                here = slots.at[kv_head, peer]
-                pltpu.make_async_copy(here, here, recv.at[kv_head, peer]).wait()
-        maxima = [stat_slots[kv_head, b] for b in range(n_blk)]
+            here = sum_slots.at[kv_head, peer]
+            pltpu.make_async_copy(here, here, sum_recv.at[kv_head, peer]).wait()
+        slots = [sum_slots[kv_head, b].astype(jnp.float32) for b in range(n_blk)]
+        maxima = [
+            sum(x[stack + i : stack + i + 1] for i in range(PARTS)) for x in slots
+        ]
         totals = [pltpu.roll(x, LANES // 2, 1) for x in maxima]
         top = functools.reduce(jnp.maximum, maxima)
         factors = [jnp.exp(x - top) for x in maxima]
@@ -204,11 +210,10 @@
             share = jnp.sum(
                 jnp.where(max_place, factors[b] / overall, 0.0), axis=1, keepdims=True
             )
-            merged = merged + sum_slots[kv_head, b].astype(jnp.float32) * share
+            merged = merged + slots[b][:stack] * share
         attention = jnp.concatenate(
             [merged[g * rows : (g + 1) * rows] for g in range(group_width)], axis=1
         ).astype(jnp.bfloat16)
-        weight_copies[kv_head].wait()
         part = pl.ds(kv_head * depth, depth)
         for chunk in range(COLUMN_CHUNKS):
             where = pl.ds(chunk * width, width)
@@ -222,13 +227,6 @@
                 continue
             for h in range(n_head):
                 terms_ref[chunk, h] = term[h * requests : (h + 1) * requests]
-            own_copy = pltpu.make_async_copy(
-                terms_ref.at[chunk, my_head],
-                parts_hbm.at[chunk, my_head],
-                term_send.at[chunk, 0],
-            )
-            own_copy.start()
-            term_copies.append(own_copy)
             for step in range(1, n_head):
                 peer = lax.rem(my_head + step, n_head)
                 copy = pltpu.make_async_remote_copy(
@@ -241,12 +239,19 @@
                 )
                 copy.start()
                 term_copies.append(copy)
-
-    for copy in term_copies:
-        copy.wait()
+            own_copy = pltpu.make_async_copy(
+                terms_ref.at[chunk, my_head],
+                parts_hbm.at[chunk, my_head],
+                term_send.at[chunk, 0],
+            )
+            own_copy.start()
+            term_copies.append(own_copy)
+
     for copies in [query_copies] + partial_copies:
         for copy in copies:
             copy.wait_send()
+    for copy in term_copies:
+        copy.wait()
 
 
 def fused(queries, stored_cache_keys, stored_cache_values, out_weight, lengths):
@@ -273,16 +278,15 @@
             pltpu.VMEM((requests * span, kv_width), jnp.bfloat16),
             pltpu.VMEM((requests * span, kv_width), jnp.bfloat16),
             pltpu.VMEM((inputs, columns), jnp.bfloat16),
-            pltpu.VMEM((local_heads, n_blk, stack, HEAD_DIMENSION), jnp.bfloat16),
-            pltpu.VMEM((local_heads, n_blk, 1, LANES), jnp.float32),
+            pltpu.VMEM(
+                (local_heads, n_blk, stack + TILE_ROWS, HEAD_DIMENSION), jnp.bfloat16
+            ),
             pltpu.VMEM((rows, columns), jnp.float32),
             pltpu.VMEM((COLUMN_CHUNKS, n_head, requests, width), jnp.float32),
             pltpu.SemaphoreType.DMA((4,)),
             pltpu.SemaphoreType.DMA((local_heads,)),
             pltpu.SemaphoreType.DMA((n_blk,)),
             pltpu.SemaphoreType.DMA((n_blk,)),
-            pltpu.SemaphoreType.DMA((local_heads, n_blk)),
-            pltpu.SemaphoreType.DMA((local_heads, n_blk)),
             pltpu.SemaphoreType.DMA((local_heads, n_blk)),
             pltpu.SemaphoreType.DMA((local_heads, n_blk)),
             pltpu.SemaphoreType.DMA((COLUMN_CHUNKS, n_head)),

time: 19 us -> 18.7 us (0.984)
  Pallas kernels: 18.1 us -> 17.9 us
    pallas_call x1, Pallas kernels: 18.1 us -> 17.9 us  [fused(): pl.pallas_call(functools.partial(fused_kernel, dims), out_shape=jax.Shape...]
where the time goes in v5:
time: 18.7 us; the launch traced here: 18.5 us
  Pallas kernels  17.9 us (96%)
  other arithmetic  0.63 us (3%)
    pallas_call x1, Pallas kernels, fused(): pl.pallas_call(functools.partial(fused_kernel, dims), out_shape=jax.Shape...  17.9 us
    reduce_sum x1, other arithmetic, fused(): summed = jnp.sum(parts, axis=1).astype(jnp.bfloat16)  0.63 us

profile of v5, /device:TPU:0, one launch (start us, length us, event | category | flops | bytes accessed | tf_op | source)
XLA Modules:
  0.0 18.5 jit_solution(11379027307682038309)
XLA Ops:
  0.0 17.9 %shard_map.55 = f32[1,4,2,2048]{3,2,1,0:T(2,128)S(1)} custom-call(s32[2]{0:T(128)} %lengths_hbm.1, bf16[2,2048]{1,0:T(2,128)(2,1)} %bitcast.8, bf16[1024,256]{1,0:T(8,128)(2,1)} %bitcast.6, bf16[1024,256]{1,0:T(8,128)(2,1)} %bitcast.7, bf16[2048,2048]{1,0:T(8,128)(2,1)} %weight_hbm.1), custom_call_target="tpu_custom_call" | custom-call | tf_op jit(solution)/shard_map/pallas_call | solution.py:268
  17.9 0.6 %reduce_sum.9 = bf16[2,2048]{1,0:T(2,128)(2,1)} reduce(f32[1,4,2,2048]{3,2,1,0:T(2,128)S(1)} %shard_map.55, f32[]{:T(128)} %constant.0.clone.1), dimensions={0,1}, to_apply=%region_0.0 | reduce | flops 12288 | bytes 73732 | tf_op jit(solution)/shard_map/reduce_sum | solution.py:308

commit v6 on v5

--- a/solution.py
+++ b/solution.py
@@ -31,7 +31,7 @@
     keys_hbm,
     values_hbm,
     weight_hbm,
-    parts_hbm,
+    parts_ref,
     lengths_ref,
     query_slots,
     keys_ref,
@@ -231,7 +231,7 @@
                 peer = lax.rem(my_head + step, n_head)
                 copy = pltpu.make_async_remote_copy(
                     src_ref=terms_ref.at[chunk, peer],
-                    dst_ref=parts_hbm.at[chunk, my_head],
+                    dst_ref=parts_ref.at[chunk, my_head],
                     send_sem=term_send.at[chunk, step],
                     recv_sem=term_recv.at[chunk, step],
                     device_id={"head": peer},
@@ -239,13 +239,7 @@
                 )
                 copy.start()
                 term_copies.append(copy)
-            own_copy = pltpu.make_async_copy(
-                terms_ref.at[chunk, my_head],
-                parts_hbm.at[chunk, my_head],
-                term_send.at[chunk, 0],
-            )
-            own_copy.start()
-            term_copies.append(own_copy)
+            parts_ref[chunk, my_head] = terms_ref[chunk, my_head]
 
     for copies in [query_copies] + partial_copies:
         for copy in copies:
@@ -271,7 +265,7 @@
             (COLUMN_CHUNKS, n_head, requests, width), jnp.float32
         ),
         in_specs=[hbm] * 5,
-        out_specs=hbm,
+        out_specs=pl.BlockSpec(memory_space=pltpu.VMEM),
         scratch_shapes=[
             pltpu.SMEM((requests,), jnp.int32),
             pltpu.VMEM((n_blk, requests, inputs), jnp.bfloat16),

time: 18.7 us -> 18.7 us (level)
  no operation moved by 1% of the time
where the time goes in v6:
time: 18.7 us; the launch traced here: 18.5 us
  Pallas kernels  17.9 us (96%)
  other arithmetic  0.63 us (3%)
    pallas_call x1, Pallas kernels, fused(): pl.pallas_call(functools.partial(fused_kernel, dims), out_shape=jax.Shape...  17.9 us
    reduce_sum x1, other arithmetic, fused(): summed = jnp.sum(parts, axis=1).astype(jnp.bfloat16)  0.63 us

profile of v6, /device:TPU:0, one launch (start us, length us, event | category | flops | bytes accessed | tf_op | source)
XLA Modules:
  0.0 18.5 jit_solution(16370513099144314021)
XLA Ops:
  0.0 17.9 %shard_map.55 = f32[1,4,2,2048]{3,2,1,0:T(2,128)S(1)} custom-call(s32[2]{0:T(128)} %lengths_hbm.1, bf16[2,2048]{1,0:T(2,128)(2,1)} %bitcast.8, bf16[1024,256]{1,0:T(8,128)(2,1)} %bitcast.6, bf16[1024,256]{1,0:T(8,128)(2,1)} %bitcast.7, bf16[2048,2048]{1,0:T(8,128)(2,1)} %weight_hbm.1), custom_call_target="tpu_custom_call" | custom-call | tf_op jit(solution)/shard_map/pallas_call | solution.py:262
  17.9 0.6 %reduce_sum.9 = bf16[2,2048]{1,0:T(2,128)(2,1)} reduce(f32[1,4,2,2048]{3,2,1,0:T(2,128)S(1)} %shard_map.55, f32[]{:T(128)} %constant.0.clone.1), dimensions={0,1}, to_apply=%region_0.0 | reduce | flops 12288 | bytes 73732 | tf_op jit(solution)/shard_map/reduce_sum | solution.py:302
